TPU v7x, 32 devices: a whole 2x2x4 slice. The times are simulated.
32 devices in a mesh: sec: 2 (over y), gy: 4 (over z), gx: 4 (over x, core).
Axes of the slice: x: 2, y: 2, z: 4, core: 2. Of those that a mesh axis runs over, the one named last changes fastest.
Arguments:
- ocean: bfloat16 [32, 3, 1024, 1536], P(('sec', 'gy'), None, None, 'gx'), may hold values from -6 to 6
- level_weight: float32 [32], replicated, may hold values from 0.25 to 2.5
- velocity_start: float32 [2, 1024, 1536], P(None, ('sec', 'gy'), 'gx'), may hold values from -3 to 3
- wind_stress: float32 [2, 1024, 1536], P(None, ('sec', 'gy'), 'gx'), may hold values from -3 to 3
- thickness: float32 [1024, 1536], P(('sec', 'gy'), 'gx'), may hold values from 0.5 to 2.5
- concentration: float32 [1024, 1536], P(('sec', 'gy'), 'gx'), may hold values from 0.3 to 1
- ice_mask: int32 [1024, 1536], P(('sec', 'gy'), 'gx'), may hold values 0 or 1
- land_mask: int32 [1024, 1536], P(('sec', 'gy'), 'gx'), may hold values 0 or 1
Outputs:
- ice_velocity: float32 [2, 1024, 1536], P(None, ('sec', 'gy'), 'gx')
- ice_stress: float32 [3, 1024, 1536], P(None, ('sec', 'gy'), 'gx')
All inputs are finite; a program needn't handle non-finite values. No bound on the sum of `ice_mask` or of `land_mask` on one device may be relied on, other than what follows from the above.
Results may differ from a plain program's by a relative error of at most 0.0003.
Values may be sent and summed in bfloat16 or wider, within the bound.
A program may use at most 128 MiB of HBM per device.

v0:
```python
import functools
import math

import jax
import jax.numpy as jnp
from jax import lax
from jax.experimental import pallas as pl
from jax.experimental.pallas import tpu as pltpu
from jax.sharding import PartitionSpec as P

SUB = 4
HALO = 8
CHUNKS = 4
PLAIN = 3
VMEM_OUT = 8 * 1024 * 1024
LANES = 128
MESH = pl.DeviceIdType.MESH

U, V, WX, WY, MASS, GRIP = range(6)
FIELDS = 6


def chunk_order():
    return [0, CHUNKS - 1] + list(range(1, CHUNKS - 1))


def numbered(secs, rows_g):
    order = chunk_order()
    others, cross = range(1, secs), range(2, rows_g)
    sends, gets = {}, {}
    for q in order:
        for i in others:
            for t in [0] + ([1] if q in order[:PLAIN] else []) + list(cross):
                sends["y", i, t, q] = len(sends)
                gets["y", i, t, q] = len(gets)
            if q in order[PLAIN:]:
                sends["a", i, q] = len(sends)
                gets["a", i, q] = len(gets)
        sends["p", q] = len(sends)
        gets["p", q] = len(gets)
        for t in cross:
            sends["c", t, q] = len(sends)
            gets["x", t, q] = len(gets)
        for m in range(1, rows_g // 2):
            gets["z", m, q] = len(gets)
    return sends, gets


def kernel(
    dims,
    weight_hbm,
    ocean_hbm,
    vel_hbm,
    wind_hbm,
    thick_hbm,
    conc_hbm,
    ice_hbm,
    land_hbm,
    fields,
    stress,
    ocean,
    send_codes,
    send_scales,
    recv_codes,
    recv_scales,
    vel_in,
    wind_in,
    thick_in,
    conc_in,
    ice_in,
    land_in,
    surf,
    ns_field_send,
    ns_field,
    ew_send,
    ew_recv,
    ns_surf_send,
    ns_surf,
    side_send,
    side_recv,
    edge_send,
    edge_recv,
    weight_ref,
    weight_sem,
    first_sems,
    ocean_sems,
    static_sems,
    send_sems,
    recv_sems,
    ns_sems,
    ew_sems,
    surf_sems,
    side_sends_sem,
    side_sems,
    edge_sems,
    gate,
):
    secs, rows_g, cols_g, levels = dims
    held = ocean_hbm.shape[0]
    tile_rows, tile_cols = thick_hbm.shape
    tiles = tile_cols // LANES
    top = 2 * HALO
    end = top + tile_rows
    size = tile_rows // CHUNKS
    pairs = rows_g // 2
    s, g, x = lax.axis_index("sec"), lax.axis_index("gy"), lax.axis_index("gx")
    ranks = secs * rows_g
    rank = s * rows_g + g
    pair = g // 2
    odd = lax.rem(g, 2)

    def at_rank(number):
        number = lax.rem(number + ranks, ranks)
        return (number // rows_g, lax.rem(number, rows_g), x)

    def row_of(t):
        if t == 0:
            return g
        if t == 1:
            return g + 1 - 2 * odd
        return 2 * lax.rem(pair + t // 2, pairs) + t % 2

    north, south = at_rank(rank - 1), at_rank(rank + 1)
    west = (s, g, lax.rem(x + cols_g - 1, cols_g))
    east = (s, g, lax.rem(x + 1, cols_g))
    over_secs = [(lax.rem(s + i, secs), g, x) for i in range(1, secs)]
    mate = (s, row_of(1), x)
    others = range(1, secs)
    cross = range(2, rows_g)
    order = chunk_order()
    traded = order[PLAIN:]
    sends, gets = numbered(secs, rows_g)

    weight_copy = pltpu.make_async_copy(weight_hbm, weight_ref, weight_sem)
    weight_copy.start()
    reads = {}

    def read(key, i, t, first, count, sem):
        block = lax.rem(s + i, secs) * rows_g + row_of(t)
        at = pl.ds(pl.multiple_of(block * tile_rows + first, 16), count)
        copy = pltpu.make_async_copy(
            ocean_hbm.at[:, :, at, :],
            ocean.at[i * rows_g + t, :, :, pl.ds(first, count), :],
            sem,
        )
        copy.start()
        reads[key] = copy

    def read_whole(i, t):
        read((i, t), i, t, 0, tile_rows, ocean_sems.at[i * rows_g + t])

    for i in others:
        for t in cross:
            read((i, t, 0), i, t, 0, size, first_sems.at[i - 1, t - 2])

    def greet(semaphore, devices):
        for device in devices + over_secs:
            pl.semaphore_signal(semaphore, inc=1, device_id=device, device_id_type=MESH)

        @pl.when(g > 0)
        def _():
            above = (s, g - 1, x)
            pl.semaphore_signal(semaphore, inc=1, device_id=above, device_id_type=MESH)

        @pl.when(g < rows_g - 1)
        def _():
            below = (s, g + 1, x)
            pl.semaphore_signal(semaphore, inc=1, device_id=below, device_id_type=MESH)

    in_line = jnp.where(g > 0, 1, 0) + jnp.where(g < rows_g - 1, 1, 0)
    barrier = pltpu.get_barrier_semaphore()
    greet(barrier, [west, east])
    weight_copy.wait()
    own_weights = [weight_ref[rank * held + k] for k in range(held)]
    strips = size // 16

    def need(i, t, q):
        key = (i, t, 0) if q == 0 and (i, t, 0) in firsts else (i, t)
        if key in reads:
            reads.pop(key).wait()

    firsts = set(reads)
    static_copies = []

    def read_rest():
        for i in others:
            for t in cross:
                read((i, t), i, t, size, tile_rows - size, ocean_sems.at[i * rows_g + t])
        for i in others:
            read_whole(i, 1)
        read_whole(0, 1)
        for i in others:
            read_whole(i, 0)
        for t in cross:
            read_whole(0, t)
        for n, (source, target) in enumerate(
            (
                (vel_hbm, vel_in),
                (wind_hbm, wind_in),
                (thick_hbm, thick_in),
                (conc_hbm, conc_in),
                (ice_hbm, ice_in),
                (land_hbm, land_in),
            )
        ):
            copy = pltpu.make_async_copy(source, target, static_sems.at[n])
            copy.start()
            static_copies.append(copy)
        read_whole(0, 0)

    def remote(source, target, send_sem, recv_sem, device):
        return pltpu.make_async_remote_copy(
            src_ref=source,
            dst_ref=target,
            send_sem=send_sem,
            recv_sem=recv_sem,
            device_id=device,
            device_id_type=MESH,
        )

    def message(send, get, device):
        return (
            remote(
                send_codes.at[send], recv_codes.at[get], send_sems.at[0], recv_sems.at[get, 0], device
            ),
            remote(
                send_scales.at[send], recv_scales.at[get], send_sems.at[1], recv_sems.at[get, 1], device
            ),
        )

    def start(copies):
        for copy in copies:
            copy.start()

    def arrived(get):
        for copy in message(0, get, mate):
            copy.wait_recv()
        return recv_codes.at[get], recv_scales.at[get]

    def level_sum(i, t, q, c, at, j):
        rows = pl.ds(q * size + at.start, 16)
        cols = pl.ds(j * LANES, LANES)
        slot = i * rows_g + t
        value = own_weights[0] * ocean[slot, 0, c, rows, cols].astype(jnp.float32)
        for k in range(1, held):
            value = value + own_weights[k] * ocean[slot, k, c, rows, cols].astype(jnp.float32)
        return value

    def decoded(codes, scale, c, at, j):
        code = codes[c, at, pl.ds(j * LANES, LANES)].astype(jnp.int32)
        return code.astype(jnp.float32) * scale

    def summed(i, t, q, received):
        def parts(c):
            scales = [scale[pl.ds(c, 1), :] for _, scale in received]

            def value_of(at, j):
                value = level_sum(i, t, q, c, at, j)
                for (codes, _), scale in zip(received, scales):
                    value = value + decoded(codes, scale, c, at, j)
                return value

            return value_of

        return parts

    def coded(parts, send):
        for c in range(3):
            value_of = parts(c)
            values = {}
            most = None
            for n in range(strips):
                at = pl.ds(n * 16, 16)
                for j in range(tiles):
                    value = value_of(at, j)
                    values[n, j] = value
                    size_of = jnp.abs(value)
                    most = size_of if most is None else jnp.maximum(most, size_of)
            most = jnp.maximum(jnp.max(most, axis=0, keepdims=True), 1e-30)
            send_scales[send, pl.ds(c, 1), :] = most * (1.0 / 32767.0)
            inverse = 32767.0 / most
            for (n, j), value in values.items():
                code = jnp.round(value * inverse)
                send_codes[send, c, pl.ds(n * 16, 16), pl.ds(j * LANES, LANES)] = code.astype(
                    jnp.int32
                ).astype(jnp.int16)

    def send_y(i, t, q, received):
        need(i, t, q)
        coded(summed(i, t, q, received), sends["y", i, t, q])

    def start_y(i, t, q):
        start(message(sends["y", i, t, q], gets["y", i, t, q], over_secs[i - 1]))

    def send_p(q):
        need(0, 1, q)
        received = []
        if q not in traded:
            received = [arrived(gets["y", i, 1, q]) for i in others]
        coded(summed(0, 1, q, received), sends["p", q])
        start(message(sends["p", q], gets["p", q], mate))

    def send_a(q):
        for i in others:
            need(i, 1, q)
            coded(summed(i, 1, q, []), sends["a", i, q])
            start(message(sends["a", i, q], gets["a", i, q], mate))

    floods = rows_g - 1
    flooded = 0

    def flood_to(number):
        nonlocal flooded
        while flooded < number:
            pl.semaphore_wait(gate.at[flooded], secs - 1 + in_line)
            flooded += 1
            if flooded < floods:
                greet(gate.at[flooded], [])

    plan = []
    for n, q in enumerate(order):
        plan.append([(t, q) for t in cross])
        if n:
            plan.append([(t, order[n - 1]) for t in (1, 0) if order[n - 1] not in traded])
    plan.append([(t, order[-1]) for t in (1, 0) if order[-1] not in traded])
    begun = False
    for n, group in enumerate(plan):
        if n:
            flood_to(min(n, floods))
        if n == 2:
            for q in traded:
                send_a(q)
            for q in traded:
                send_p(q)
        for t, q in group:
            for i in others:
                send_y(i, t, q, [])
                if not begun:
                    read_rest()
                    pl.semaphore_wait(barrier, secs + 1 + in_line)
                start_y(i, t, q)
                if not begun:
                    greet(gate.at[0], [])
                    begun = True
    flood_to(floods)

    has_north, has_south = rank > 0, rank < ranks - 1

    def rows_up(source, target, sems):
        return remote(
            source.at[0], target.at[1], sems.at[0, 0], sems.at[0, 1], north
        )

    def rows_down(source, target, sems):
        return remote(
            source.at[1],
            target.at[0],
            sems.at[1, 0],
            sems.at[1, 1],
            south,
        )

    def either(condition, yes, no):
        pl.when(condition)(yes)
        pl.when(jnp.logical_not(condition))(no)

    def place_rows(target, received, count, side, has, waits):
        to = pl.ds(end, HALO) if side else pl.ds(HALO, HALO)

        def there():
            waits()
            for f in range(count):
                for j in range(tiles):
                    target[f, j, to, :] = received[side, f, j]

        def missing():
            for f in range(count):
                for j in range(tiles):
                    target[f, j, to, :] = jnp.zeros((HALO, LANES), jnp.float32)

        either(has, there, missing)

    lane = lax.broadcasted_iota(jnp.int32, (8, LANES), 1)
    all_strips = (tile_rows + 2 * HALO) // 8

    def beyond(west_value, east_value):
        return jnp.where(
            lane < HALO, east_value, jnp.where(lane >= LANES - HALO, west_value, 0.0)
        )

    per_piece = LANES // HALO

    def edges_of(ref, places):
        out = []
        for j, offset in ((0, 0), (tiles - 1, HALO)):
            packed = [jnp.zeros((8, LANES), jnp.float32)] * pl.cdiv(len(places), per_piece)
            for n, (c, row) in enumerate(places):
                piece, spot = divmod(n, per_piece)
                value = ref[c, j, pl.ds(row, 8), :]
                shift = (spot * HALO + offset) % LANES
                value = pltpu.roll(value, shift, 1) if shift else value
                packed[piece] = jnp.where(lane // HALO == spot, value, packed[piece])
            out.append(packed)
        return out

    def place_edges(ref, places, west_values, east_values):
        for n, (c, row) in enumerate(places):
            piece, spot = divmod(n, per_piece)
            back = (LANES - HALO - spot * HALO) % LANES
            from_west = west_values[piece]
            from_west = pltpu.roll(from_west, back, 1) if back else from_west
            back = (LANES - spot * HALO) % LANES
            from_east = east_values[piece]
            from_east = pltpu.roll(from_east, back, 1) if back else from_east
            ref[c, tiles, pl.ds(row, 8), :] = beyond(from_west, from_east)

    def sideways(sends, gets, sems):
        return (
            remote(sends.at[0], gets.at[1], sems.at[0, 0], sems.at[0, 1], west),
            remote(sends.at[1], gets.at[0], sems.at[1, 0], sems.at[1, 1], east),
        )

    field_columns = sideways(ew_send, ew_recv, ew_sems)
    field_places = [(f, HALO + 8 * n) for f in range(FIELDS) for n in range(all_strips)]
    field_pieces = range(ew_recv.shape[1])
    every = tiles + 1
    relay = {t: (row_of(t) > g) == (odd == 1) for t in cross}

    def cross_message(t, q, relaying):
        @pl.when(relay[t] if relaying else jnp.logical_not(relay[t]))
        def _():
            received = [arrived(gets["y", i, t, q]) for i in others]
            send = sends["c", t, q]
            if relaying:
                received.append(arrived(gets["x", t, q]))
            coded(summed(0, t, q, received), send)
            if relaying:
                start(message(send, gets["z", t // 2, q], (s, row_of(t), x)))
            else:
                start(message(send, gets["x", t, q], mate))

    def statics():
        for copy in static_copies:
            copy.wait()

        @pl.loop(0, tile_rows // 8)
        def _(i):
            at = pl.ds(pl.multiple_of(i * 8, 8), 8)
            to = pl.ds(pl.multiple_of(i * 8 + top, 8), 8)
            for j in range(tiles):
                cols = pl.ds(j * LANES, LANES)
                for f in range(2):
                    fields[U + f, j, to, :] = vel_in[f, at, cols]
                    fields[WX + f, j, to, :] = wind_in[f, at, cols]
                thick = thick_in[at, cols]
                ice = ice_in[at, cols].astype(jnp.float32)
                strength = jnp.exp(-4.0 * (1.0 - conc_in[at, cols])) * thick
                fields[GRIP, j, to, :] = strength * ice * (1.0 / 3.0)
                fields[MASS, j, to, :] = thick * (ice * land_in[at, cols].astype(jnp.float32))

        for f in range(FIELDS):
            for j in range(tiles):
                ns_field_send[0, f, j] = fields[f, j, pl.ds(top, HALO), :]
                ns_field_send[1, f, j] = fields[f, j, pl.ds(end - HALO, HALO), :]

        @pl.when(has_north)
        def _():
            rows_up(ns_field_send, ns_field, ns_sems).start()

        @pl.when(has_south)
        def _():
            rows_down(ns_field_send, ns_field, ns_sems).start()

    def field_halo():
        place_rows(
            fields, ns_field, FIELDS, 0, has_north,
            lambda: rows_down(ns_field_send, ns_field, ns_sems).wait_recv(),
        )
        place_rows(
            fields, ns_field, FIELDS, 1, has_south,
            lambda: rows_up(ns_field_send, ns_field, ns_sems).wait_recv(),
        )

        @pl.when(has_north)
        def _():
            rows_up(ns_field_send, ns_field, ns_sems).wait_send()

        @pl.when(has_south)
        def _():
            rows_down(ns_field_send, ns_field, ns_sems).wait_send()

        for side, packed in enumerate(edges_of(fields, field_places)):
            for piece, value in enumerate(packed):
                ew_send[side, piece] = value
        start(field_columns)

    def margins(target, count):
        zero = jnp.zeros((8, LANES), jnp.float32)
        for f in range(count):
            for j in range(every):
                target[f, j, pl.ds(0, HALO), :] = zero
                target[f, j, pl.ds(end + HALO, HALO), :] = zero

    def sides(values):
        before = [pltpu.roll(value, 1, 1) for value in values]
        after = [pltpu.roll(value, LANES - 1, 1) for value in values]
        out = []
        for j in range(every):
            low = jnp.where(lane == 0, before[j - 1], before[j])
            high = jnp.where(lane == LANES - 1, after[(j + 1) % every], after[j])
            out.append(0.5 * (high - low))
        return out

    def strip_rows(i, shift):
        if shift == 0:
            return pl.ds(pl.multiple_of(i * 8 + HALO, 8), 8)
        return pl.ds(i * 8 + HALO + shift, 8)

    def rows_of(ref, f, at):
        return [ref[f, j, at, :] for j in range(every)]

    def stress_step(first):
        @pl.loop(0, all_strips, unroll=True)
        def _(i):
            at, up, down = strip_rows(i, 0), strip_rows(i, -1), strip_rows(i, 1)
            east_u = sides(rows_of(fields, U, at))
            east_v = sides(rows_of(fields, V, at))
            for j in range(every):
                north_u = 0.5 * (fields[U, j, down, :] - fields[U, j, up, :])
                north_v = 0.5 * (fields[V, j, down, :] - fields[V, j, up, :])
                spread = east_u[j] + north_v
                tension = east_u[j] - north_v
                shear = north_u + east_v[j]
                turned = lax.rsqrt(
                    spread * spread + 0.25 * (tension * tension + shear * shear) + 0.01
                )
                grip = fields[GRIP, j, at, :]
                rate = grip * turned
                new0 = rate * spread - grip
                new1 = (0.25 * rate) * tension
                new2 = (0.125 * rate) * shear
                if not first:
                    new0 = stress[0, j, at, :] * (1.0 / 1.5) + new0
                    new1 = stress[1, j, at, :] * (1.0 / 1.5) + new1
                    new2 = stress[2, j, at, :] * (1.0 / 1.5) + new2
                stress[0, j, at, :] = new0
                stress[1, j, at, :] = new1
                stress[2, j, at, :] = new2

    def velocity_step(first_strip=0, last_strip=all_strips, width=tiles + 1):
        @pl.loop(first_strip, last_strip, unroll=True)
        def _(i):
            at, up, down = strip_rows(i, 0), strip_rows(i, -1), strip_rows(i, 1)
            first = rows_of(stress, 0, at)
            second = rows_of(stress, 1, at)
            east_normal = sides([0.5 * (a + b) for a, b in zip(first, second)])
            east_third = sides(rows_of(stress, 2, at))
            for j in range(width):
                north_third = 0.5 * (stress[2, j, down, :] - stress[2, j, up, :])
                north_normal = 0.25 * (
                    (stress[0, j, down, :] - stress[1, j, down, :])
                    - (stress[0, j, up, :] - stress[1, j, up, :])
                )
                u, v = fields[U, j, at, :], fields[V, j, at, :]
                cx, cy = surf[0, j, at, :], surf[1, j, at, :]
                mass = fields[MASS, j, at, :]
                rel_u, rel_v = cx - u, cy - v
                drag = 0.8 * jnp.sqrt(rel_u * rel_u + rel_v * rel_v)
                a = mass + drag
                b = 0.5 * mass
                rx = mass * u + (east_normal[j] + north_third) + drag * cx + fields[WX, j, at, :]
                ry = mass * v + (east_third[j] + north_normal) + drag * cy + fields[WY, j, at, :]
                live = mass > 0.0
                inverse = 1.0 / jnp.where(live, a * a + b * b, 1.0)
                fields[U, j, at, :] = jnp.where(live, (a * rx + b * ry) * inverse, 0.0)
                fields[V, j, at, :] = jnp.where(live, (a * ry - b * rx) * inverse, 0.0)

    def first_stress():
        for copy in field_columns:
            copy.wait()
        place_edges(
            fields,
            field_places,
            [ew_recv[0, piece] for piece in field_pieces],
            [ew_recv[1, piece] for piece in field_pieces],
        )
        margins(fields, 2)
        margins(stress, 3)
        margins(surf, 3)
        stress_step(True)

    norm = 1.0 / math.sqrt(levels)
    chunk_strips = size // 8
    pieces = side_send.shape[2]
    first_rows, last_rows = pl.ds(top, HALO), pl.ds(end - HALO, HALO)

    def up_halo():
        return remote(
            ns_surf_send.at[0], ns_surf.at[1], surf_sems.at[0, 0], surf_sems.at[0, 1], north
        )

    def down_halo():
        return remote(
            ns_surf_send.at[1], ns_surf.at[0], surf_sems.at[1, 0], surf_sems.at[1, 1], south
        )

    def inside(q):
        return [(c, top + q * size + 8 * n) for c in range(3) for n in range(chunk_strips)]

    outside = [(c, row) for c in range(3) for row in (HALO, end)]

    def side_copies(q):
        return (
            remote(side_send.at[q, 0], side_recv.at[q, 1], side_sends_sem, side_sems.at[q, 1], west),
            remote(side_send.at[q, 1], side_recv.at[q, 0], side_sends_sem, side_sems.at[q, 0], east),
        )

    def surface(q):
        need(0, 0, q)
        received = [arrived(gets["y", i, 0, q]) for i in others]
        received.append(arrived(gets["p", q]))
        received += [arrived(gets["z", m, q]) for m in range(1, pairs)]
        parts = summed(0, 0, q, received)
        for c in range(3):
            value_of = parts(c)
            for n in range(strips):
                for j in range(tiles):
                    to = pl.ds(top + q * size + n * 16, 16)
                    surf[c, j, to, :] = value_of(pl.ds(n * 16, 16), j) * norm
        for side, packed in enumerate(edges_of(surf, inside(q))):
            for piece in range(pieces):
                side_send[q, side, piece] = packed[piece]
        start(side_copies(q))
        for side, edge, rows in ((0, 0, first_rows), (1, CHUNKS - 1, last_rows)):
            if q == edge:
                for c in range(3):
                    for j in range(tiles):
                        ns_surf_send[side, c, j] = surf[c, j, rows, :]
        if q == 0:

            @pl.when(has_north)
            def _():
                up_halo().start()

        if q == CHUNKS - 1:

            @pl.when(has_south)
            def _():
                down_halo().start()

    def place_halo(side, has, wait):
        to = pl.ds(end, HALO) if side else pl.ds(HALO, HALO)

        def there():
            wait()
            for c in range(3):
                for j in range(tiles):
                    surf[c, j, to, :] = ns_surf[side, c, j]

        def missing():
            for c in range(3):
                for j in range(tiles):
                    surf[c, j, to, :] = jnp.zeros((HALO, LANES), jnp.float32)

        either(has, there, missing)

    edge_copies = sideways(edge_send, edge_recv, edge_sems)

    def surface_halo():
        place_halo(0, has_north, lambda: down_halo().wait_recv())
        place_halo(1, has_south, lambda: up_halo().wait_recv())

        @pl.when(has_north)
        def _():
            up_halo().wait_send()

        @pl.when(has_south)
        def _():
            down_halo().wait_send()

        for side, packed in enumerate(edges_of(surf, outside)):
            edge_send[side] = packed[0]
        start(edge_copies)

    def surface_sides(q):
        for copy in side_copies(q):
            copy.wait_recv()
        place_edges(
            surf,
            inside(q),
            [side_recv[q, 0, piece] for piece in range(pieces)],
            [side_recv[q, 1, piece] for piece in range(pieces)],
        )

    for n, q in enumerate(order):
        for t in cross:
            need(0, t, q)
            cross_message(t, q, False)
        if n and order[n - 1] not in traded:
            send_p(order[n - 1])
        for t in cross:
            cross_message(t, q, True)
        if n == 0:
            statics()
            for late in traded:
                for i in others:
                    send_y(i, 0, late, [arrived(gets["a", i, late])])
                    start_y(i, 0, late)
        if n == 2:
            field_halo()
        if n >= 2:
            surface(order[n - 2])
    if order[-1] not in traded:
        send_p(order[-1])
    first_stress()
    surface(order[-2])
    for q in order[:-2]:
        surface_sides(q)
    surface_halo()
    surface_sides(order[-2])
    for send_sem, source in ((send_sems.at[0], send_codes), (send_sems.at[1], send_scales)):
        remote(source, source, send_sem, recv_sems.at[0, 0], mate).wait_send()
    surface(order[-1])
    for copy in edge_copies:
        copy.wait()
    place_edges(surf, outside, [edge_recv[0]], [edge_recv[1]])
    surface_sides(order[-1])
    remote(side_send, side_recv, side_sends_sem, side_sems.at[0, 0], west).wait_send()

    @pl.loop(0, all_strips, unroll=True)
    def _(i):
        at, up, down = strip_rows(i, 0), strip_rows(i, -1), strip_rows(i, 1)
        slope_x = sides(rows_of(surf, 2, at))
        for j in range(every):
            slope_y = 0.5 * (surf[2, j, down, :] - surf[2, j, up, :])
            gain = -0.5 * fields[MASS, j, at, :]
            fields[WX, j, at, :] = fields[WX, j, at, :] + gain * slope_x[j]
            fields[WY, j, at, :] = fields[WY, j, at, :] + gain * slope_y

    velocity_step()

    @pl.loop(0, SUB - 2)
    def _(cycle):
        stress_step(False)
        velocity_step()

    stress_step(False)
    velocity_step(1, all_strips - 1, tiles)

def write_out(fields, stress, vel_out, stress_out, sems):
    tiles = fields.shape[1] - 1
    rows = pl.ds(2 * HALO, vel_out.shape[1])
    copies = []
    for j in range(tiles):
        cols = pl.ds(j * LANES, LANES)
        for n, (source, target) in enumerate(
            ((fields.at[pl.ds(U, 2)], vel_out), (stress, stress_out))
        ):
            copy = pltpu.make_async_copy(
                source.at[:, j, rows, :], target.at[:, :, cols], sems.at[n, j]
            )
            copy.start()
            copies.append(copy)
    for copy in copies:
        copy.wait()


def body(
    ocean, level_weight, velocity_start, wind_stress, thickness, concentration, ice_mask, land_mask
):
    secs, rows_g, cols_g = lax.axis_size("sec"), lax.axis_size("gy"), lax.axis_size("gx")
    held = ocean.shape[0]
    rows, cols = thickness.shape
    tiles = cols // LANES
    tall = rows + 4 * HALO
    wide_rows = rows + 2 * HALO
    size = rows // CHUNKS
    pieces = pl.cdiv(3 * (size // 8), LANES // HALO)
    field_pieces = pl.cdiv(FIELDS * (wide_rows // 8), LANES // HALO)
    f32, i16 = jnp.float32, jnp.int16
    dma = pltpu.SemaphoreType.DMA
    anywhere = pl.BlockSpec(memory_space=pl.ANY)
    on_chip = pl.BlockSpec(memory_space=pltpu.VMEM)
    sends, gets = numbered(secs, rows_g)
    fields, stress = pl.pallas_call(
        functools.partial(kernel, (secs, rows_g, cols_g, level_weight.shape[0])),
        out_shape=(
            pltpu.VMEM((FIELDS, tiles + 1, tall, LANES), f32),
            pltpu.VMEM((3, tiles + 1, tall, LANES), f32),
        ),
        in_specs=[anywhere] * 8,
        out_specs=(on_chip, on_chip),
        scratch_shapes=[
            pltpu.VMEM((secs * rows_g, held, 3, rows, cols), ocean.dtype),
            pltpu.VMEM((len(sends), 3, size, cols), i16),
            pltpu.VMEM((len(sends), 3, LANES), f32),
            pltpu.VMEM((len(gets), 3, size, cols), i16),
            pltpu.VMEM((len(gets), 3, LANES), f32),
            pltpu.VMEM((2, rows, cols), f32),
            pltpu.VMEM((2, rows, cols), f32),
            pltpu.VMEM((rows, cols), f32),
            pltpu.VMEM((rows, cols), f32),
            pltpu.VMEM((rows, cols), jnp.int32),
            pltpu.VMEM((rows, cols), jnp.int32),
            pltpu.VMEM((3, tiles + 1, tall, LANES), f32),
            pltpu.VMEM((2, FIELDS, tiles, HALO, LANES), f32),
            pltpu.VMEM((2, FIELDS, tiles, HALO, LANES), f32),
            pltpu.VMEM((2, field_pieces, 8, LANES), f32),
            pltpu.VMEM((2, field_pieces, 8, LANES), f32),
            pltpu.VMEM((2, 3, tiles, HALO, LANES), f32),
            pltpu.VMEM((2, 3, tiles, HALO, LANES), f32),
            pltpu.VMEM((CHUNKS, 2, pieces, 8, LANES), f32),
            pltpu.VMEM((CHUNKS, 2, pieces, 8, LANES), f32),
            pltpu.VMEM((2, 8, LANES), f32),
            pltpu.VMEM((2, 8, LANES), f32),
            pltpu.SMEM(level_weight.shape, f32),
            dma(()),
            dma((secs - 1, rows_g - 2)),
            dma((secs * rows_g,)),
            dma((6,)),
            dma((2,)),
            dma((len(gets), 2)),
            dma((2, 2)),
            dma((2, 2)),
            dma((2, 2)),
            dma(()),
            dma((CHUNKS, 2)),
            dma((2, 2)),
            pltpu.SemaphoreType.REGULAR((rows_g - 1,)),
        ],
        compiler_params=pltpu.CompilerParams(
            collective_id=0, has_side_effects=True, vmem_limit_bytes=52 * 1024 * 1024
        ),
    )(
        level_weight,
        ocean,
        velocity_start,
        wind_stress,
        thickness,
        concentration,
        ice_mask,
        land_mask,
    )
    return pl.pallas_call(
        write_out,
        out_shape=(
            jax.ShapeDtypeStruct((2, rows, cols), f32),
            jax.ShapeDtypeStruct((3, rows, cols), f32),
        ),
        in_specs=[on_chip, on_chip],
        out_specs=(anywhere, anywhere),
        scratch_shapes=[dma((2, tiles))],
        compiler_params=pltpu.CompilerParams(vmem_limit_bytes=VMEM_OUT),
    )(fields, stress)


def solution(mesh):
    placed = (
        P(("sec", "gy"), None, None, "gx"),
        P(),
        P(None, ("sec", "gy"), "gx"),
        P(None, ("sec", "gy"), "gx"),
        P(("sec", "gy"), "gx"),
        P(("sec", "gy"), "gx"),
        P(("sec", "gy"), "gx"),
        P(("sec", "gy"), "gx"),
    )
    return jax.shard_map(
        body,
        mesh=mesh,
        in_specs=placed,
        out_specs=(P(None, ("sec", "gy"), "gx"), P(None, ("sec", "gy"), "gx")),
        check_vma=False,
    )
```

profile of v0, /device:TPU:1, one launch (start us, length us, event | category | flops | bytes accessed | tf_op | source)
XLA Modules:
  0.0 43.6 jit_solution(11872492267196017236)
XLA Ops:
  0.6 41.9 %shard_map.95 = (f32[6,4,160,128]{3,2,1,0:T(8,128)S(1)}, f32[3,4,160,128]{3,2,1,0:T(8,128)S(1)}) custom-call(f32[32]{0:T(128)} %weight_hbm.1, bf16[4,3,1024,384]{3,2,1,0:T(8,128)(2,1)} %ocean_hbm.1, f32[2,128,384]{2,1,0:T(8,128)} %vel_hbm.1, f32[2,128,384]{2,1,0:T(8,128)} %wind_hbm.1, f32[128,384]{1,0:T(8,128)} %thick_hbm.1, f32[128,384]{1,0:T(8,128)} %conc_hbm.1, ...), custom_call_target="tpu_custom_call" | custom-call | tf_op jit(solution)/shard_map/pallas_call | solution.py:785
  42.6 1.0 %shard_map.96 = (f32[2,128,384]{2,1,0:T(8,128)}, f32[3,128,384]{2,1,0:T(8,128)}) custom-call(f32[6,4,160,128]{3,2,1,0:T(8,128)S(1)} %get-tuple-element.4.fields, f32[3,4,160,128]{3,2,1,0:T(8,128)S(1)} %get-tuple-element.5.stress), custom_call_target="tpu_custom_call" | custom-call | tf_op jit(solution)/shard_map/pallas_call | solution.py:844
where the time goes:
time: 43.9 us; the launch traced here: 43.6 us
  Pallas kernels  42.9 us (98%)
  between operations  0.64 us (1%)
    pallas_call x1, Pallas kernels, body(): pl.pallas_call(functools.partial(kernel, (secs, rows_g, cols_g, level_wei...  41.9 us
    pallas_call x1, Pallas kernels, body(): pl.pallas_call(write_out, out_shape=(jax.ShapeDtypeStruct((2, rows, cols)...  0.99 us

commit v1 on v0

--- a/solution.py
+++ b/solution.py
@@ -12,6 +12,7 @@
 HALO = 8
 CHUNKS = 4
 PLAIN = 3
+LEAD = 2
 VMEM_OUT = 8 * 1024 * 1024
 LANES = 128
 MESH = pl.DeviceIdType.MESH
@@ -70,16 +71,17 @@
     ice_in,
     land_in,
     surf,
-    ns_field_send,
-    ns_field,
+    ns_codes,
+    ns_scales,
+    ns_got,
+    ns_scales_got,
     ew_send,
     ew_recv,
     ns_surf_send,
     ns_surf,
     side_send,
     side_recv,
-    edge_send,
-    edge_recv,
+    corner_recv,
     weight_ref,
     weight_sem,
     first_sems,
@@ -92,7 +94,6 @@
     surf_sems,
     side_sends_sem,
     side_sems,
-    edge_sems,
     gate,
 ):
     secs, rows_g, cols_g, levels = dims
@@ -123,6 +124,8 @@
     north, south = at_rank(rank - 1), at_rank(rank + 1)
     west = (s, g, lax.rem(x + cols_g - 1, cols_g))
     east = (s, g, lax.rem(x + 1, cols_g))
+    north_west, north_east = north[:2] + west[2:], north[:2] + east[2:]
+    south_west, south_east = south[:2] + west[2:], south[:2] + east[2:]
     over_secs = [(lax.rem(s + i, secs), g, x) for i in range(1, secs)]
     mate = (s, row_of(1), x)
     others = range(1, secs)
@@ -306,23 +309,25 @@
             coded(summed(i, 1, q, []), sends["a", i, q])
             start(message(sends["a", i, q], gets["a", i, q], mate))
 
-    floods = rows_g - 1
+    floods = rows_g
     flooded = 0
 
     def flood_to(number):
         nonlocal flooded
         while flooded < number:
-            pl.semaphore_wait(gate.at[flooded], secs - 1 + in_line)
+            pl.semaphore_wait(gate.at[flooded], secs + 1 + in_line)
             flooded += 1
             if flooded < floods:
-                greet(gate.at[flooded], [])
-
-    plan = []
+                greet(gate.at[flooded], [west, east])
+
+    plan = [[(t, q) for t in cross] for q in order[:LEAD]]
     for n, q in enumerate(order):
-        plan.append([(t, q) for t in cross])
-        if n:
-            plan.append([(t, order[n - 1]) for t in (1, 0) if order[n - 1] not in traded])
-    plan.append([(t, order[-1]) for t in (1, 0) if order[-1] not in traded])
+        if n + LEAD < len(order):
+            plan.append([(1, q)] * (q not in traded))
+            plan.append([(t, order[n + LEAD]) for t in cross])
+            plan.append([(0, q)] * (q not in traded))
+        else:
+            plan.append([(t, q) for t in (1, 0)] * (q not in traded))
     begun = False
     for n, group in enumerate(plan):
         if n:
@@ -340,43 +345,63 @@
                     pl.semaphore_wait(barrier, secs + 1 + in_line)
                 start_y(i, t, q)
                 if not begun:
-                    greet(gate.at[0], [])
+                    greet(gate.at[0], [west, east])
                     begun = True
     flood_to(floods)
 
     has_north, has_south = rank > 0, rank < ranks - 1
 
-    def rows_up(source, target, sems):
-        return remote(
-            source.at[0], target.at[1], sems.at[0, 0], sems.at[0, 1], north
+    def rows_up():
+        return (
+            remote(ns_codes.at[0], ns_got.at[1], ns_sems.at[0, 0, 0], ns_sems.at[0, 0, 1], north),
+            remote(ns_scales.at[0], ns_scales_got.at[1], ns_sems.at[0, 1, 0], ns_sems.at[0, 1, 1], north),
         )
 
-    def rows_down(source, target, sems):
-        return remote(
-            source.at[1],
-            target.at[0],
-            sems.at[1, 0],
-            sems.at[1, 1],
-            south,
+    def rows_down():
+        return (
+            remote(ns_codes.at[1], ns_got.at[0], ns_sems.at[1, 0, 0], ns_sems.at[1, 0, 1], south),
+            remote(ns_scales.at[1], ns_scales_got.at[0], ns_sems.at[1, 1, 0], ns_sems.at[1, 1, 1], south),
         )
+
+    def pack_rows(side):
+        rows = pl.ds(end - HALO, HALO) if side else pl.ds(top, HALO)
+        for f in range(0, FIELDS, 2):
+            inverses = []
+            for k in (f, f + 1):
+                most = jnp.abs(fields[k, 0, rows, :])
+                for j in range(1, tiles):
+                    most = jnp.maximum(most, jnp.abs(fields[k, j, rows, :]))
+                most = jnp.maximum(jnp.max(most, axis=0, keepdims=True), 1e-30)
+                ns_scales[side, pl.ds(k, 1), :] = most * (1.0 / 32767.0)
+                inverses.append(jnp.broadcast_to(32767.0 / most, (HALO, LANES)))
+            inverse = jnp.concatenate(inverses, axis=0)
+            for j in range(tiles):
+                value = jnp.concatenate([fields[f, j, rows, :], fields[f + 1, j, rows, :]], axis=0)
+                code = jnp.round(value * inverse).astype(jnp.int32).astype(jnp.int16)
+                ns_codes[side, pl.ds(f * HALO, 2 * HALO), pl.ds(j * LANES, LANES)] = code
 
     def either(condition, yes, no):
         pl.when(condition)(yes)
         pl.when(jnp.logical_not(condition))(no)
 
-    def place_rows(target, received, count, side, has, waits):
+    def place_rows(side, has, copies):
         to = pl.ds(end, HALO) if side else pl.ds(HALO, HALO)
 
         def there():
-            waits()
-            for f in range(count):
+            for copy in copies():
+                copy.wait_recv()
+            for f in range(0, FIELDS, 2):
+                scales = [ns_scales_got[side, pl.ds(k, 1), :] for k in (f, f + 1)]
                 for j in range(tiles):
-                    target[f, j, to, :] = received[side, f, j]
+                    code = ns_got[side, pl.ds(f * HALO, 2 * HALO), pl.ds(j * LANES, LANES)]
+                    value = code.astype(jnp.int32).astype(jnp.float32)
+                    fields[f, j, to, :] = value[0:HALO] * scales[0]
+                    fields[f + 1, j, to, :] = value[HALO : 2 * HALO] * scales[1]
 
         def missing():
-            for f in range(count):
+            for f in range(FIELDS):
                 for j in range(tiles):
-                    target[f, j, to, :] = jnp.zeros((HALO, LANES), jnp.float32)
+                    fields[f, j, to, :] = jnp.zeros((HALO, LANES), jnp.float32)
 
         either(has, there, missing)
 
@@ -458,36 +483,30 @@
                 fields[GRIP, j, to, :] = strength * ice * (1.0 / 3.0)
                 fields[MASS, j, to, :] = thick * (ice * land_in[at, cols].astype(jnp.float32))
 
-        for f in range(FIELDS):
-            for j in range(tiles):
-                ns_field_send[0, f, j] = fields[f, j, pl.ds(top, HALO), :]
-                ns_field_send[1, f, j] = fields[f, j, pl.ds(end - HALO, HALO), :]
+        pack_rows(0)
+        pack_rows(1)
 
         @pl.when(has_north)
         def _():
-            rows_up(ns_field_send, ns_field, ns_sems).start()
+            start(rows_up())
 
         @pl.when(has_south)
         def _():
-            rows_down(ns_field_send, ns_field, ns_sems).start()
+            start(rows_down())
 
     def field_halo():
-        place_rows(
-            fields, ns_field, FIELDS, 0, has_north,
-            lambda: rows_down(ns_field_send, ns_field, ns_sems).wait_recv(),
-        )
-        place_rows(
-            fields, ns_field, FIELDS, 1, has_south,
-            lambda: rows_up(ns_field_send, ns_field, ns_sems).wait_recv(),
-        )
+        place_rows(0, has_north, rows_down)
+        place_rows(1, has_south, rows_up)
 
         @pl.when(has_north)
         def _():
-            rows_up(ns_field_send, ns_field, ns_sems).wait_send()
+            for copy in rows_up():
+                copy.wait_send()
 
         @pl.when(has_south)
         def _():
-            rows_down(ns_field_send, ns_field, ns_sems).wait_send()
+            for copy in rows_down():
+                copy.wait_send()
 
         for side, packed in enumerate(edges_of(fields, field_places)):
             for piece, value in enumerate(packed):
@@ -519,8 +538,8 @@
     def rows_of(ref, f, at):
         return [ref[f, j, at, :] for j in range(every)]
 
-    def stress_step(first):
-        @pl.loop(0, all_strips, unroll=True)
+    def stress_step(first, low, high):
+        @pl.loop(low, high, unroll=True)
         def _(i):
             at, up, down = strip_rows(i, 0), strip_rows(i, -1), strip_rows(i, 1)
             east_u = sides(rows_of(fields, U, at))
@@ -547,8 +566,8 @@
                 stress[1, j, at, :] = new1
                 stress[2, j, at, :] = new2
 
-    def velocity_step(first_strip=0, last_strip=all_strips, width=tiles + 1):
-        @pl.loop(first_strip, last_strip, unroll=True)
+    def velocity_step(low, high, width):
+        @pl.loop(low, high, unroll=True)
         def _(i):
             at, up, down = strip_rows(i, 0), strip_rows(i, -1), strip_rows(i, 1)
             first = rows_of(stress, 0, at)
@@ -587,27 +606,36 @@
         margins(fields, 2)
         margins(stress, 3)
         margins(surf, 3)
-        stress_step(True)
+        stress_step(True, 0, all_strips)
 
     norm = 1.0 / math.sqrt(levels)
     chunk_strips = size // 8
     pieces = side_send.shape[2]
     first_rows, last_rows = pl.ds(top, HALO), pl.ds(end - HALO, HALO)
 
-    def up_halo():
-        return remote(
-            ns_surf_send.at[0], ns_surf.at[1], surf_sems.at[0, 0], surf_sems.at[0, 1], north
-        )
-
-    def down_halo():
-        return remote(
-            ns_surf_send.at[1], ns_surf.at[0], surf_sems.at[1, 0], surf_sems.at[1, 1], south
-        )
+    def halo(side):
+        sent, got = ns_surf_send.at[side], ns_surf.at[1 - side]
+        devices = (south, south_west, south_east) if side else (north, north_west, north_east)
+        return [
+            remote(sent, got, surf_sems.at[side, 0, 0], surf_sems.at[side, 0, 1], devices[0]),
+            remote(
+                sent.at[:, 0],
+                corner_recv.at[1 - side, 1],
+                surf_sems.at[side, 1, 0],
+                surf_sems.at[side, 1, 1],
+                devices[1],
+            ),
+            remote(
+                sent.at[:, tiles - 1],
+                corner_recv.at[1 - side, 0],
+                surf_sems.at[side, 2, 0],
+                surf_sems.at[side, 2, 1],
+                devices[2],
+            ),
+        ]
 
     def inside(q):
         return [(c, top + q * size + 8 * n) for c in range(3) for n in range(chunk_strips)]
-
-    outside = [(c, row) for c in range(3) for row in (HALO, end)]
 
     def side_copies(q):
         return (
@@ -640,47 +668,45 @@
 
             @pl.when(has_north)
             def _():
-                up_halo().start()
+                start(halo(0))
 
         if q == CHUNKS - 1:
 
             @pl.when(has_south)
             def _():
-                down_halo().start()
-
-    def place_halo(side, has, wait):
+                start(halo(1))
+
+    def place_halo(side, has):
         to = pl.ds(end, HALO) if side else pl.ds(HALO, HALO)
 
         def there():
-            wait()
+            for copy in halo(1 - side):
+                copy.wait_recv()
             for c in range(3):
                 for j in range(tiles):
                     surf[c, j, to, :] = ns_surf[side, c, j]
+                surf[c, tiles, to, :] = beyond(corner_recv[side, 0, c], corner_recv[side, 1, c])
 
         def missing():
             for c in range(3):
-                for j in range(tiles):
+                for j in range(every):
                     surf[c, j, to, :] = jnp.zeros((HALO, LANES), jnp.float32)
 
         either(has, there, missing)
 
-    edge_copies = sideways(edge_send, edge_recv, edge_sems)
-
     def surface_halo():
-        place_halo(0, has_north, lambda: down_halo().wait_recv())
-        place_halo(1, has_south, lambda: up_halo().wait_recv())
+        place_halo(0, has_north)
+        place_halo(1, has_south)
 
         @pl.when(has_north)
         def _():
-            up_halo().wait_send()
+            for copy in halo(0):
+                copy.wait_send()
 
         @pl.when(has_south)
         def _():
-            down_halo().wait_send()
-
-        for side, packed in enumerate(edges_of(surf, outside)):
-            edge_send[side] = packed[0]
-        start(edge_copies)
+            for copy in halo(1):
+                copy.wait_send()
 
     def surface_sides(q):
         for copy in side_copies(q):
@@ -691,6 +717,44 @@
             [side_recv[q, 0, piece] for piece in range(pieces)],
             [side_recv[q, 1, piece] for piece in range(pieces)],
         )
+
+    def slope_step(low, high):
+        @pl.loop(low, high, unroll=True)
+        def _(i):
+            at, up, down = strip_rows(i, 0), strip_rows(i, -1), strip_rows(i, 1)
+            slope_x = sides(rows_of(surf, 2, at))
+            for j in range(every):
+                slope_y = 0.5 * (surf[2, j, down, :] - surf[2, j, up, :])
+                gain = -0.5 * fields[MASS, j, at, :]
+                fields[WX, j, at, :] = fields[WX, j, at, :] + gain * slope_x[j]
+                fields[WY, j, at, :] = fields[WY, j, at, :] + gain * slope_y
+
+    halves = 2 * SUB - 1
+
+    def half_step(h, low, high):
+        if h == halves - 1:
+            low, high = max(low, 1), min(high, all_strips - 1)
+        low, high = max(low, 0), min(high, all_strips)
+        if low >= high:
+            return
+        if h == 0:
+            slope_step(low, high)
+        if h % 2:
+            stress_step(False, low, high)
+        else:
+            velocity_step(low, high, tiles if h == halves - 1 else every)
+
+    late_low = 1 + order[-1] * chunk_strips - 1
+    late_high = 1 + (order[-1] + 1) * chunk_strips + 1
+
+    def early_steps(first, last):
+        for h in range(first, last):
+            half_step(h, 0, late_low - h)
+            half_step(h, late_high + h, all_strips)
+
+    def late_steps():
+        for h in range(halves):
+            half_step(h, late_low - h, late_high + h)
 
     for n, q in enumerate(order):
         for t in cross:
@@ -706,7 +770,7 @@
                 for i in others:
                     send_y(i, 0, late, [arrived(gets["a", i, late])])
                     start_y(i, 0, late)
-        if n == 2:
+        if n == CHUNKS // 2:
             field_halo()
         if n >= 2:
             surface(order[n - 2])
@@ -716,36 +780,16 @@
     surface(order[-2])
     for q in order[:-2]:
         surface_sides(q)
-    surface_halo()
     surface_sides(order[-2])
     for send_sem, source in ((send_sems.at[0], send_codes), (send_sems.at[1], send_scales)):
         remote(source, source, send_sem, recv_sems.at[0, 0], mate).wait_send()
     surface(order[-1])
-    for copy in edge_copies:
-        copy.wait()
-    place_edges(surf, outside, [edge_recv[0]], [edge_recv[1]])
+    surface_halo()
+    early_steps(0, halves)
     surface_sides(order[-1])
+    late_steps()
     remote(side_send, side_recv, side_sends_sem, side_sems.at[0, 0], west).wait_send()
 
-    @pl.loop(0, all_strips, unroll=True)
-    def _(i):
-        at, up, down = strip_rows(i, 0), strip_rows(i, -1), strip_rows(i, 1)
-        slope_x = sides(rows_of(surf, 2, at))
-        for j in range(every):
-            slope_y = 0.5 * (surf[2, j, down, :] - surf[2, j, up, :])
-            gain = -0.5 * fields[MASS, j, at, :]
-            fields[WX, j, at, :] = fields[WX, j, at, :] + gain * slope_x[j]
-            fields[WY, j, at, :] = fields[WY, j, at, :] + gain * slope_y
-
-    velocity_step()
-
-    @pl.loop(0, SUB - 2)
-    def _(cycle):
-        stress_step(False)
-        velocity_step()
-
-    stress_step(False)
-    velocity_step(1, all_strips - 1, tiles)
 
 def write_out(fields, stress, vel_out, stress_out, sems):
     tiles = fields.shape[1] - 1
@@ -803,16 +847,17 @@
             pltpu.VMEM((rows, cols), jnp.int32),
             pltpu.VMEM((rows, cols), jnp.int32),
             pltpu.VMEM((3, tiles + 1, tall, LANES), f32),
-            pltpu.VMEM((2, FIELDS, tiles, HALO, LANES), f32),
-            pltpu.VMEM((2, FIELDS, tiles, HALO, LANES), f32),
+            pltpu.VMEM((2, FIELDS * HALO, cols), i16),
+            pltpu.VMEM((2, FIELDS, LANES), f32),
+            pltpu.VMEM((2, FIELDS * HALO, cols), i16),
+            pltpu.VMEM((2, FIELDS, LANES), f32),
             pltpu.VMEM((2, field_pieces, 8, LANES), f32),
             pltpu.VMEM((2, field_pieces, 8, LANES), f32),
             pltpu.VMEM((2, 3, tiles, HALO, LANES), f32),
             pltpu.VMEM((2, 3, tiles, HALO, LANES), f32),
             pltpu.VMEM((CHUNKS, 2, pieces, 8, LANES), f32),
             pltpu.VMEM((CHUNKS, 2, pieces, 8, LANES), f32),
-            pltpu.VMEM((2, 8, LANES), f32),
-            pltpu.VMEM((2, 8, LANES), f32),
+            pltpu.VMEM((2, 2, 3, HALO, LANES), f32),
             pltpu.SMEM(level_weight.shape, f32),
             dma(()),
             dma((secs - 1, rows_g - 2)),
@@ -820,13 +865,12 @@
             dma((6,)),
             dma((2,)),
             dma((len(gets), 2)),
+            dma((2, 2, 2)),
             dma((2, 2)),
-            dma((2, 2)),
-            dma((2, 2)),
+            dma((2, 3, 2)),
             dma(()),
             dma((CHUNKS, 2)),
-            dma((2, 2)),
-            pltpu.SemaphoreType.REGULAR((rows_g - 1,)),
+            pltpu.SemaphoreType.REGULAR((rows_g,)),
         ],
         compiler_params=pltpu.CompilerParams(
             collective_id=0, has_side_effects=True, vmem_limit_bytes=52 * 1024 * 1024

time: 43.9 us -> 42.5 us (0.968)
  Pallas kernels: 42.9 us -> 41.7 us
    pallas_call x1, Pallas kernels: 41.9 us -> 40.7 us  [body(): pl.pallas_call(functools.partial(kernel, (secs, rows_g, cols_g, level_wei...]
where the time goes in v1:
time: 42.5 us; the launch traced here: 42.4 us
  Pallas kernels  41.7 us (98%)
  between operations  0.64 us (2%)
    pallas_call x1, Pallas kernels, body(): pl.pallas_call(functools.partial(kernel, (secs, rows_g, cols_g, level_wei...  40.7 us
    pallas_call x1, Pallas kernels, body(): pl.pallas_call(write_out, out_shape=(jax.ShapeDtypeStruct((2, rows, cols)...  0.99 us

profile of v1, /device:TPU:1, one launch (start us, length us, event | category | flops | bytes accessed | tf_op | source)
XLA Modules:
  0.0 42.4 jit_solution(17615621076879431900)
XLA Ops:
  0.6 40.7 %shard_map.95 = (f32[6,4,160,128]{3,2,1,0:T(8,128)S(1)}, f32[3,4,160,128]{3,2,1,0:T(8,128)S(1)}) custom-call(f32[32]{0:T(128)} %weight_hbm.1, bf16[4,3,1024,384]{3,2,1,0:T(8,128)(2,1)} %ocean_hbm.1, f32[2,128,384]{2,1,0:T(8,128)} %vel_hbm.1, f32[2,128,384]{2,1,0:T(8,128)} %wind_hbm.1, f32[128,384]{1,0:T(8,128)} %thick_hbm.1, f32[128,384]{1,0:T(8,128)} %conc_hbm.1, ...), custom_call_target="tpu_custom_call" | custom-call | tf_op jit(solution)/shard_map/pallas_call | solution.py:829
  41.4 1.0 %shard_map.96 = (f32[2,128,384]{2,1,0:T(8,128)}, f32[3,128,384]{2,1,0:T(8,128)}) custom-call(f32[6,4,160,128]{3,2,1,0:T(8,128)S(1)} %get-tuple-element.4.fields, f32[3,4,160,128]{3,2,1,0:T(8,128)S(1)} %get-tuple-element.5.stress), custom_call_target="tpu_custom_call" | custom-call | tf_op jit(solution)/shard_map/pallas_call | solution.py:888

commit v2 on v1

--- a/solution.py
+++ b/solution.py
@@ -11,7 +11,7 @@
 SUB = 4
 HALO = 8
 CHUNKS = 4
-PLAIN = 3
+PLAIN = 4
 LEAD = 2
 VMEM_OUT = 8 * 1024 * 1024
 LANES = 128

time: 42.5 us -> 43.1 us (1.014)
  Pallas kernels: 41.7 us -> 42.3 us
    pallas_call x1, Pallas kernels: 40.7 us -> 41.3 us  [body(): pl.pallas_call(functools.partial(kernel, (secs, rows_g, cols_g, level_wei...]
where the time goes in v2:
time: 43.1 us; the launch traced here: 43 us
  Pallas kernels  42.3 us (98%)
  between operations  0.64 us (1%)
    pallas_call x1, Pallas kernels, body(): pl.pallas_call(functools.partial(kernel, (secs, rows_g, cols_g, level_wei...  41.3 us
    pallas_call x1, Pallas kernels, body(): pl.pallas_call(write_out, out_shape=(jax.ShapeDtypeStruct((2, rows, cols)...  0.99 us

profile of v2, /device:TPU:1, one launch (start us, length us, event | category | flops | bytes accessed | tf_op | source)
XLA Modules:
  0.0 43.0 jit_solution(3795904357438052521)
XLA Ops:
  0.6 41.3 %shard_map.95 = (f32[6,4,160,128]{3,2,1,0:T(8,128)S(1)}, f32[3,4,160,128]{3,2,1,0:T(8,128)S(1)}) custom-call(f32[32]{0:T(128)} %weight_hbm.1, bf16[4,3,1024,384]{3,2,1,0:T(8,128)(2,1)} %ocean_hbm.1, f32[2,128,384]{2,1,0:T(8,128)} %vel_hbm.1, f32[2,128,384]{2,1,0:T(8,128)} %wind_hbm.1, f32[128,384]{1,0:T(8,128)} %thick_hbm.1, f32[128,384]{1,0:T(8,128)} %conc_hbm.1, ...), custom_call_target="tpu_custom_call" | custom-call | tf_op jit(solution)/shard_map/pallas_call | solution.py:829
  42.0 1.0 %shard_map.96 = (f32[2,128,384]{2,1,0:T(8,128)}, f32[3,128,384]{2,1,0:T(8,128)}) custom-call(f32[6,4,160,128]{3,2,1,0:T(8,128)S(1)} %get-tuple-element.4.fields, f32[3,4,160,128]{3,2,1,0:T(8,128)S(1)} %get-tuple-element.5.stress), custom_call_target="tpu_custom_call" | custom-call | tf_op jit(solution)/shard_map/pallas_call | solution.py:888
